TPU v7x, 256 devices: a whole 4x4x8 slice. The times are simulated.
256 devices in a mesh: leaf: 64 (over x, z, core), front: 4 (over y).
Axes of the slice: x: 4, y: 4, z: 8, core: 2. Of those that a mesh axis runs over, the one named last changes fastest.
Arguments:
- child_update: bfloat16 [64, 4, 1, 3, 256, 3072], P('leaf', 'front'), may hold values from -60 to 60, as said below
- sep_one: bfloat16 [64, 4, 1, 4, 256, 512], P('leaf', 'front'), may hold values from -60 to 60, as said below
- sep_two: bfloat16 [64, 4, 1, 4, 256, 256], P('leaf', 'front'), may hold values from -60 to 60, as said below
- map_one: int32 [64, 1, 4, 3], replicated, may hold values from 0 to 3, as said below
- map_two: int32 [32, 1, 4, 3], replicated, may hold values from 0 to 3, as said below
- mask_one: int32 [32, 1, 12, 4], replicated, may hold values 0 or 1
- mask_two: int32 [16, 1, 12, 4], replicated, may hold values 0 or 1
Outputs:
- factor_one: float32 [64, 4, 1, 4, 256, 512], P('leaf', 'front')
- factor_two: float32 [64, 4, 1, 4, 256, 256], P('leaf', 'front')
- update_two: bfloat16 [64, 4, 1, 3, 256, 768], P('leaf', 'front')
Inputs may be any that keep to these rules, and one draw needn't show every extreme that they name: `child_update`: every child[l,b] is symmetric positive definite. `sep_one`: the top 1024 rows of each front's initial entries form a symmetric positive definite block, and every assembled front is positive definite. `sep_two`: the top 1024 rows of each front's initial entries form a symmetric positive definite block, and every assembled front is positive definite. `map_one`: for each child, batch and j the 3 entries are distinct; the two children 2p and 2p + 1 leave out different slots, so every parent tile receives one or two child tiles. `map_two`: for each first-level front, batch and j the 3 entries are distinct; fronts 2q and 2q + 1 leave out different slots, so every parent tile receives one or two child tiles.
All inputs are finite; a program needn't handle non-finite values.
Results may differ from a plain program's by a relative error of at most 0.0047.
Values may be sent and summed in bfloat16 or wider, within the bound.
A program may use at most 192 MiB of HBM per device.

v0:
```python
import jax
import jax.numpy as jnp
from jax import lax
from jax.sharding import PartitionSpec as P

TILE = 256
ST = 4
UT = 12
FT = 16
S = 1024
U = 3072
F = 4096


def swapped(value, axis, apart):
    mask = 2**apart
    pairs = [(source, source ^ mask) for source in range(lax.axis_size(axis))]
    return lax.ppermute(value, axis, pairs)


def place_tiles(blocks, row_source, row_live, col_source, col_live):
    taken = jnp.take(blocks, row_source, axis=0)
    taken = jnp.take(taken, col_source, axis=2)
    keep = jnp.logical_and(row_live[:, None, None, None], col_live[None, None, :, None])
    return jnp.where(keep, taken.astype(jnp.float32), 0.0)


def place_child(child_rows, tile_map, column):
    batch_count = child_rows.shape[0]
    local_tiles = child_rows.shape[1]
    groups = tile_map.shape[1]
    slot_count = FT // groups
    own_slots = lax.dynamic_index_in_dim(tile_map, column, 1, keepdims=False)
    row_hit = own_slots[..., None] == jnp.arange(slot_count, dtype=jnp.int32)
    row_source = jnp.sum(
        row_hit.astype(jnp.int32) * jnp.arange(local_tiles, dtype=jnp.int32)[None, :, None], axis=1
    )
    row_live = jnp.any(row_hit, axis=1)
    targets = (jnp.swapaxes(tile_map, 1, 2) * groups + jnp.arange(groups, dtype=jnp.int32)).reshape(
        batch_count, UT
    )
    col_hit = targets[..., None] == jnp.arange(FT, dtype=jnp.int32)
    col_source = jnp.sum(
        col_hit.astype(jnp.int32) * jnp.arange(UT, dtype=jnp.int32)[None, :, None], axis=1
    )
    col_live = jnp.any(col_hit, axis=1)
    blocks = child_rows.reshape(batch_count, local_tiles, TILE, UT, TILE)
    placed = jax.vmap(place_tiles)(blocks, row_source, row_live, col_source, col_live)
    return placed.reshape(batch_count, slot_count, TILE, F)


def join_halves(mine, other, position):
    lower_first = jnp.concatenate([mine, other], axis=-1)
    upper_first = jnp.concatenate([other, mine], axis=-1)
    return jnp.where(position == 0, lower_first, upper_first)


def add_initial(canvas, initial, mask_front, column):
    batch_count = canvas.shape[0]
    slot_count = canvas.shape[1]
    groups = lax.axis_size("front")
    mask_rows = mask_front.reshape(batch_count, slot_count - 1, groups, ST)
    mask_rows = lax.dynamic_index_in_dim(mask_rows, column, 2, keepdims=False).astype(jnp.float32)
    mask_all = jnp.concatenate([jnp.ones((batch_count, 1, ST), jnp.float32), mask_rows], axis=1)
    weighted = initial.astype(jnp.float32).reshape(batch_count, slot_count, TILE, ST, TILE)
    weighted = (weighted * mask_all[:, :, None, :, None]).reshape(batch_count, slot_count, TILE, S)
    return jnp.concatenate([canvas[:, :, :, :S] + weighted, canvas[:, :, :, S:]], axis=-1)


def factor_front(canvas, column):
    batch_count = canvas.shape[0]
    local_tiles = canvas.shape[1] - 1
    groups = lax.axis_size("front")
    pivot_piece = canvas[:, :1, :, :S]
    pivot_all = lax.all_gather(pivot_piece[None], "front", axis=0, tiled=True)
    pivot_block = jnp.moveaxis(pivot_all, 0, 2).reshape(batch_count, S, S)
    lower_factor = jnp.linalg.cholesky(pivot_block)
    coupling = canvas[:, 1:, :, :S].reshape(batch_count, local_tiles * TILE, S)
    panel_full = lax.linalg.triangular_solve(
        lower_factor, coupling, left_side=False, lower=True, transpose_a=True
    )
    panel_round = panel_full.astype(jnp.bfloat16)
    shared = lax.all_gather(
        panel_round.reshape(batch_count, local_tiles, TILE, S)[None], "front", axis=0, tiled=True
    )
    ordered = jnp.transpose(shared, (1, 2, 0, 3, 4)).reshape(batch_count, U, S)
    own_lower = lax.dynamic_index_in_dim(
        lower_factor.reshape(batch_count, groups, TILE, S), column, 1, keepdims=True
    )
    factor_rows = jnp.concatenate(
        [own_lower, panel_full.reshape(batch_count, local_tiles, TILE, S)], axis=1
    )
    trailing = canvas[:, 1:, :, S:].reshape(batch_count, local_tiles * TILE, U)
    product = jnp.einsum("brk,bnk->brn", panel_round, ordered, preferred_element_type=jnp.float32)
    update = (trailing - product).astype(jnp.bfloat16)
    return (factor_rows, update)


def body(child_update, sep_one, sep_two, map_one, map_two, mask_one, mask_two):
    column = lax.axis_index("front")
    leaf_index = lax.axis_index("leaf")
    half_index = leaf_index % 2
    quarter_index = leaf_index % 4
    pair_index = leaf_index // 2
    quad_index = leaf_index // 4
    side_index = pair_index % 2
    child_rows = child_update[0, 0]
    batch_count = child_rows.shape[0]
    local_tiles = child_rows.shape[1]
    entries_one = sep_one[0, 0]
    entries_two = sep_two[0, 0]
    peer_rows, peer_one, peer_two = swapped((child_rows, entries_one, entries_two), "leaf", 0)
    map_own = lax.dynamic_index_in_dim(map_one, leaf_index, 0, keepdims=False)
    map_peer = lax.dynamic_index_in_dim(map_one, jnp.bitwise_xor(leaf_index, 1), 0, keepdims=False)
    front_first = place_child(child_rows, map_own, column) + place_child(
        peer_rows, map_peer, column
    )
    initial_one = join_halves(entries_one, peer_one, half_index)
    mask_front = lax.dynamic_index_in_dim(mask_one, pair_index, 0, keepdims=False)
    front_first = add_initial(front_first, initial_one, mask_front, column)
    factor_rows_one, update_one = factor_front(front_first, column)
    factor_one = lax.dynamic_slice_in_dim(factor_rows_one, half_index * (S // 2), S // 2, 3)
    entries_half = join_halves(entries_two, peer_two, quarter_index % 2)
    update_far, entries_far = swapped((update_one, entries_half), "leaf", 1)
    map_near = lax.dynamic_index_in_dim(map_two, pair_index, 0, keepdims=False)
    map_far = lax.dynamic_index_in_dim(map_two, jnp.bitwise_xor(pair_index, 1), 0, keepdims=False)
    near_rows = update_one.reshape(batch_count, local_tiles, TILE, U)
    far_rows = update_far.reshape(batch_count, local_tiles, TILE, U)
    front_second = place_child(near_rows, map_near, column) + place_child(far_rows, map_far, column)
    initial_two = join_halves(entries_half, entries_far, side_index)
    mask_second = lax.dynamic_index_in_dim(mask_two, quad_index, 0, keepdims=False)
    front_second = add_initial(front_second, initial_two, mask_second, column)
    factor_rows_two, update_last = factor_front(front_second, column)
    update_last = lax.dynamic_slice_in_dim(update_last, quarter_index * (U // 4), U // 4, 2)
    factor_two = lax.dynamic_slice_in_dim(factor_rows_two, quarter_index * (S // 4), S // 4, 3)
    update_two = update_last.reshape(batch_count, local_tiles, TILE, U // 4)
    return (factor_one[None, None], factor_two[None, None], update_two[None, None])


def solution(mesh):
    return jax.shard_map(
        body,
        mesh=mesh,
        in_specs=(
            P("leaf", "front", None, None, None, None),
            P("leaf", "front", None, None, None, None),
            P("leaf", "front", None, None, None, None),
            P(),
            P(),
            P(),
            P(),
        ),
        out_specs=(
            P("leaf", "front", None, None, None, None),
            P("leaf", "front", None, None, None, None),
            P("leaf", "front", None, None, None, None),
        ),
        check_vma=False,
    )
```

profile of v0, /device:TPU:1, one launch (start us, length us, event | category | flops | bytes accessed | tf_op | source)
XLA Modules:
  0.0 1299.8 jit_solution(7646188197757473696)
XLA Ops:
  74.5 13.8 %select_add_fusion.1 = f32[1,4,256,16,256]{4,2,1,3,0:T(8,128)} fusion(bf16[16,4,256,256]{3,2,1,0:T(8,128)(2,1)} %gather_fusion.3, bf16[16,4,256,256]{3,2,1,0:T(8,128)(2,1)} %gather_fusion.1, pred[16]{0:T(512)(128)(4,1)S(1)} %and_bitcast_fusion.4, pred[16]{0:T(512)(128)(4,1)S(1)} %and_bitcast_fusion.6, pred[4,16]{0,1:T(8,128)(4,1)S(1)} %broadcast_and_fusion.2, ...), kind=kLoop, calls=%fused_computation.13 | loop fusion | flops 29360128 | bytes 33554592 | tf_op jit(solution)/shard_map/add | solution.py:115
  88.3 16.4 %copy.145 = f32[1,4,256,16,256]{2,4,3,1,0:T(8,128)} copy(f32[1,4,256,16,256]{4,2,1,3,0:T(8,128)} %select_add_fusion.1) | data formatting | bytes 33554432 | tf_op jit(solution)/shard_map/add | solution.py:115
  116.7 47.7 %all-gather.11.cloned.1.call-done = f32[4,1,256,1024]{3,2,1,0:T(8,128)} async-done(((f32[1,1,256,1024]{3,2,1,0:T(8,128)}), f32[4,1,256,1024]{3,2,1,0:T(8,128)}) %all-gather.11.cloned.1.call-update) | async-done | bytes 4194320 | tf_op jit(solution)/shard_map/all_gather | solution.py:75
  176.6 11.7 custom-call.91
  189.0 9.8 custom-call.92
  205.2 11.9 custom-call.93
  218.3 9.8 custom-call.94
  231.5 11.7 custom-call.95
  244.5 9.8 custom-call.96
  257.9 11.9 custom-call.97
  271.1 9.8 custom-call.98
  284.4 11.7 custom-call.99
  297.5 10.2 custom-call.100
  311.0 11.7 custom-call.101
  324.0 9.8 custom-call.102
  336.8 11.9 custom-call.103
  349.9 9.8 custom-call.104
  362.3 11.7 custom-call.105
  387.9 28.1 %while.4 = (s32[]{:T(128)}, f32[1,1024,1024]{2,1,0:T(8,128)}, s32[8,2]{0,1:T(2,128)S(1)}, f32[8,1,128,128]{3,2,1,0:T(8,128)}, s32[]{:T(128)}) while((s32[]{:T(128)}, f32[1,1024,1024]{2,1,0:T(8,128)}, s32[8,2]{0,1:T(2,128)S(1)}, f32[8,1,128,128]{3,2,1,0:T(8,128)}, s32[]{:T(128)}) %tuple.131), condition=%wide.while_cond, body=%wide.while_body.sunk | while | flops 2 | bytes 132205 | solution.py:79
  416.0 80.4 %custom-call.106 = f32[1,8,128,128]{2,3,1,0:T(8,128)} custom-call(f32[1,8,128,128]{3,2,1,0:T(8,128)} %bitcast.928), custom_call_target="InvertDiagBlocksLowerTriangular" | custom-call | tf_op jit(solution)/shard_map/triangular_solve/custom-call.7 | solution.py:79
  539.8 9.8 copy.156
  549.6 50.9 %all-gather.7.cloned.1.call-done = bf16[4,1,3,256,1024]{4,3,2,1,0:T(8,128)(2,1)} async-done(((bf16[1,1,3,256,1024]{4,3,2,1,0:T(8,128)(2,1)}), bf16[4,1,3,256,1024]{4,3,2,1,0:T(8,128)(2,1)}) %all-gather.7.cloned.1.call-update) | async-done | bytes 6291472 | tf_op jit(solution)/shard_map/all_gather | solution.py:83
  618.6 9.6 reshape_reshape.6
  654.7 61.9 %collective-permute-done.2 = bf16[1,768,3072]{2,1,0:T(8,128)(2,1)} collective-permute-done((bf16[1,768,3072]{2,1,0:T(8,128)(2,1)}, bf16[1,768,3072]{2,1,0:T(8,128)(2,1)}, u32[]{:S(2)}, u32[]{:S(2)}) %collective-permute-start.2) | collective-permute-done | bytes 4718624 | tf_op jit(solution)/shard_map/ppermute | solution.py:18
  716.6 9.2 reshape_reshape.7
  752.2 13.8 %select_add_fusion = f32[1,4,256,16,256]{4,2,1,3,0:T(8,128)} fusion(bf16[16,4,256,256]{3,2,1,0:T(8,128)(2,1)} %gather_fusion.7, bf16[16,4,256,256]{3,2,1,0:T(8,128)(2,1)} %gather_fusion.5, pred[16]{0:T(512)(128)(4,1)S(1)} %and_bitcast_fusion, pred[16]{0:T(512)(128)(4,1)S(1)} %and_bitcast_fusion.2, pred[4,16]{0,1:T(8,128)(4,1)S(1)} %broadcast_and_fusion, ...), kind=kLoop, calls=%fused_computation.12 | loop fusion | flops 29360128 | bytes 33554592 | tf_op jit(solution)/shard_map/add | solution.py:129
  766.0 16.4 %copy.163 = f32[1,4,256,16,256]{2,4,3,1,0:T(8,128)} copy(f32[1,4,256,16,256]{4,2,1,3,0:T(8,128)} %select_add_fusion) | data formatting | bytes 33554432 | tf_op jit(solution)/shard_map/add | solution.py:129
  793.6 49.4 %all-gather.13.cloned.1.call-done = f32[4,1,256,1024]{3,2,1,0:T(8,128)} async-done(((f32[1,1,256,1024]{3,2,1,0:T(8,128)}), f32[4,1,256,1024]{3,2,1,0:T(8,128)}) %all-gather.13.cloned.1.call-update) | async-done | bytes 4194320 | tf_op jit(solution)/shard_map/all_gather | solution.py:75
  854.9 11.7 custom-call.111
  867.3 9.8 custom-call.112
  883.5 11.9 custom-call.113
  896.7 9.8 custom-call.114
  909.9 11.7 custom-call.115
  922.8 9.8 custom-call.116
  936.2 12.1 custom-call.117
  949.6 9.8 custom-call.118
  962.9 11.7 custom-call.119
  975.9 9.9 custom-call.120
  989.2 11.7 custom-call.121
  1002.2 9.8 custom-call.122
  1015.0 11.9 custom-call.123
  1028.2 9.8 custom-call.124
  1040.6 11.7 custom-call.125
  1066.2 28.1 %while.5 = (s32[]{:T(128)}, f32[1,1024,1024]{2,1,0:T(8,128)}, s32[8,2]{0,1:T(2,128)S(1)}, f32[8,1,128,128]{3,2,1,0:T(8,128)}, s32[]{:T(128)}) while((s32[]{:T(128)}, f32[1,1024,1024]{2,1,0:T(8,128)}, s32[8,2]{0,1:T(2,128)S(1)}, f32[8,1,128,128]{3,2,1,0:T(8,128)}, s32[]{:T(128)}) %tuple.145), condition=%wide.while_cond.clone, body=%wide.while_body.clone.sunk | while | flops 2 | bytes 132205 | solution.py:79
  1094.3 80.4 %custom-call.126 = f32[1,8,128,128]{2,3,1,0:T(8,128)} custom-call(f32[1,8,128,128]{3,2,1,0:T(8,128)} %bitcast.927), custom_call_target="InvertDiagBlocksLowerTriangular" | custom-call | tf_op jit(solution)/shard_map/triangular_solve/custom-call.7 | solution.py:79
  1219.5 8.5 slice.400
  1227.9 10.1 copy.173
  1244.0 37.3 %all-gather.9.cloned.1.call-done = bf16[4,1,3,256,1024]{4,3,2,1,0:T(8,128)(2,1)} async-done(((bf16[1,1,3,256,1024]{4,3,2,1,0:T(8,128)(2,1)}), bf16[4,1,3,256,1024]{4,3,2,1,0:T(8,128)(2,1)}) %all-gather.9.cloned.1.call-update) | async-done | bytes 6291472 | tf_op jit(solution)/shard_map/all_gather | solution.py:83
  (338 shorter events, 432.8 us)
Async XLA Ops:
  7.2 11.9 copy-start
  7.2 157.2 %all-gather.11.cloned.1.call-start = ((), (), s32[]{:S(2)}) async-start(), calls=%async_computation.2 | async-start | bytes 5242880 | tf_op jit(solution)/shard_map/all_gather | solution.py:75
  8.7 10.0 copy-start.18
  8.7 10.8 copy-start.19
  8.7 11.2 copy-start.17
  8.7 95.9 %collective-permute-start.1 = (bf16[1,4,256,512]{2,3,1,0:T(8,128)(2,1)S(1)}, bf16[1,4,256,512]{2,3,1,0:T(8,128)(2,1)S(1)}, u32[]{:S(2)}, u32[]{:S(2)}) collective-permute-start(bf16[1,4,256,512]{2,3,1,0:T(8,128)(2,1)S(1)} %bitcast.921), channel_id=1, source_target_pairs={{0,4},{4,0},{8,12},{12,8},{16,20},{20,16},{24,28},{28,24},{32,36},... | collective-permute-start | bytes 3145736 | tf_op jit(solution)/shard_map/ppermute | solution.py:18
  18.7 29.6 %collective-permute-start = (bf16[1,3,256,3072]{2,3,1,0:T(8,128)(2,1)}, bf16[1,3,256,3072]{2,3,1,0:T(8,128)(2,1)}, u32[]{:S(2)}, u32[]{:S(2)}) collective-permute-start(bf16[1,3,256,3072]{2,3,1,0:T(8,128)(2,1)} %bitcast.880), channel_id=1, source_target_pairs={{0,4},{4,0},{8,12},{12,8},{16,20},{20,16},{24,28},{28,24},{32,36},... | collective-permute-start | bytes 14155784 | tf_op jit(solution)/shard_map/ppermute | solution.py:18
  109.0 2.0 copy-start.2
  112.3 1.9 slice-start
  112.4 488.2 %all-gather.7.cloned.1.call-start = ((), (), s32[]{:S(2)}) async-start(), calls=%async_computation | async-start | bytes 7864320 | tf_op jit(solution)/shard_map/all_gather | solution.py:83
  174.6 1.9 copy-start.10
  380.3 116.2 %copy-start.9 = (f32[1,3,256,1024]{3,2,1,0:T(8,128)S(1)}, f32[1,3,256,1024]{3,2,1,0:T(8,128)}, u32[]{:S(2)}) copy-start(f32[1,3,256,1024]{3,2,1,0:T(8,128)} %copy.152) | copy-start | bytes 9437188
  496.4 6.9 copy-start.14
  528.4 1.7 copy-start.4
  531.8 311.2 %all-gather.13.cloned.1.call-start = ((), (), s32[]{:S(2)}) async-start(), calls=%async_computation.3 | async-start | bytes 5242880 | tf_op jit(solution)/shard_map/all_gather | solution.py:75
  600.5 5.5 copy-start.12
  606.0 8.9 copy-start.16
  613.7 102.9 %collective-permute-start.2 = (bf16[1,768,3072]{2,1,0:T(8,128)(2,1)}, bf16[1,768,3072]{2,1,0:T(8,128)(2,1)}, u32[]{:S(2)}, u32[]{:S(2)}) collective-permute-start(bf16[1,768,3072]{2,1,0:T(8,128)(2,1)} %bitcast.920), channel_id=1, source_target_pairs={{0,8},{4,12},{8,0},{12,4},{16,24},{20,28},{24,16},{28,20},{32,40},... | collective-permute-start | bytes 14155784 | tf_op jit(solution)/shard_map/ppermute | solution.py:18
  615.2 2.6 collective-permute-start.3
  618.0 164.3 %collective-permute-start.4 = (bf16[1,4,256,512]{2,3,1,0:T(8,128)(2,1)S(1)}, bf16[1,4,256,512]{2,3,1,0:T(8,128)(2,1)}, u32[]{:S(2)}, u32[]{:S(2)}) collective-permute-start(bf16[1,4,256,512]{2,3,1,0:T(8,128)(2,1)S(1)} %maximum_select_fusion.3), channel_id=1, source_target_pairs={{0,8},{4,12},{8,0},{12,4},{16,24},{20,28},{24,16},{28,20},{32,40},... | collective-permute-start | bytes 3145736 | tf_op jit(solution)/shard_map/ppermute | solution.py:18
  785.9 2.0 copy-start.3
  789.3 1.9 slice-start.1
  789.3 492.0 %all-gather.9.cloned.1.call-start = ((), (), s32[]{:S(2)}) async-start(), calls=%async_computation.1 | async-start | bytes 7864320 | tf_op jit(solution)/shard_map/all_gather | solution.py:83
  853.0 1.9 copy-start.11
  1058.6 116.1 %copy-start.8 = (f32[1,3,256,1024]{3,2,1,0:T(8,128)S(1)}, f32[1,3,256,1024]{3,2,1,0:T(8,128)}, u32[]{:S(2)}) copy-start(f32[1,3,256,1024]{3,2,1,0:T(8,128)} %copy.171) | copy-start | bytes 9437188
  1174.7 6.9 copy-start.15
  1206.7 1.7 copy-start.6
  1208.4 4.1 copy-start.5
  1227.9 10.1 copy-start.7
  1244.0 40.8 %copy-start.13 = (bf16[1,768,1024]{1,2,0:T(8,128)(2,1)S(1)}, bf16[1,768,1024]{1,2,0:T(8,128)(2,1)}, u32[]{:S(2)}) copy-start(bf16[1,768,1024]{1,2,0:T(8,128)(2,1)} %convert_element_type.105) | copy-start | bytes 4718596
  1284.8 8.2 copy-start.1
Sparse Core Ops, SparseCore 0:
  112.5 51.8 all-gather.10
  532.0 68.5 all-gather.6
  789.4 53.5 all-gather.12
  1212.7 68.5 all-gather.8
where the time goes:
time: 1310 us; the launch traced here: 1300 us
  other arithmetic  602 us (46%)
  local copies, waits for them, and re-layouts  297 us (23%)
  waiting for transfers between devices  248 us (19%)
  matrix products  123 us (9%)
  between operations  25 us (2%)
    another operation x62, other arithmetic, factor_front(): lower_factor = jnp.linalg.cholesky(pivot_block)  346 us
    another operation x5, other arithmetic, factor_front(): lax.linalg.triangular_solve(lower_factor, coupling, left_side=False, lowe...  174 us
    all_gather x2, waiting for transfers between devices, factor_front(): pivot_all = lax.all_gather(pivot_piece[None], 'front', axis=0, tiled=True)  97.1 us
    all_gather x2, waiting for transfers between devices, factor_front(): lax.all_gather(panel_round.reshape(batch_count, local_tiles, TILE, S)[Non...  88.2 us
    another operation x30, matrix products, factor_front(): lax.linalg.triangular_solve(lower_factor, coupling, left_side=False, lowe...  63.6 us
    another operation x53, local copies, waits for them, and re-layouts, factor_front(): lax.linalg.triangular_solve(lower_factor, coupling, left_side=False, lowe...  62.7 us
    ppermute x5, waiting for transfers between devices, swapped(): return lax.ppermute(value, axis, pairs)  62.4 us
    another operation x28, matrix products, factor_front(): lower_factor = jnp.linalg.cholesky(pivot_block)  46.3 us
  transfers between devices with their start and end apart: 9, of which 6 were waited for; matrix products, arithmetic and copies ran while one was open for 19% of the time, Pallas kernels for 0%

commit v1 on v0

--- a/solution.py
+++ b/solution.py
@@ -10,6 +10,19 @@
 S = 1024
 U = 3072
 F = 4096
+
+
+def collect(x, axis, dim):
+    ways = lax.axis_size(axis)
+    up = [(d, (d + 1) % ways) for d in range(ways)]
+    down = [(d, (d - 1) % ways) for d in range(ways)]
+    earlier, later = ([x], [x])
+    for _ in range(ways // 2):
+        earlier.append(lax.ppermute(earlier[-1], axis, up))
+    for _ in range((ways - 1) // 2):
+        later.append(lax.ppermute(later[-1], axis, down))
+    line = jnp.concatenate([*earlier[::-1], *later[1:]], axis=dim)
+    return jnp.roll(line, (lax.axis_index(axis) - ways // 2) * x.shape[dim], axis=dim)
 
 
 def swapped(value, axis, apart):
@@ -72,7 +85,7 @@
     local_tiles = canvas.shape[1] - 1
     groups = lax.axis_size("front")
     pivot_piece = canvas[:, :1, :, :S]
-    pivot_all = lax.all_gather(pivot_piece[None], "front", axis=0, tiled=True)
+    pivot_all = collect(pivot_piece[None], "front", 0)
     pivot_block = jnp.moveaxis(pivot_all, 0, 2).reshape(batch_count, S, S)
     lower_factor = jnp.linalg.cholesky(pivot_block)
     coupling = canvas[:, 1:, :, :S].reshape(batch_count, local_tiles * TILE, S)

time: 1310 us -> 1340 us (1.023)
  local copies, waits for them, and re-layouts: 297 us -> 313 us
    all_gather x2 -> x0, waiting for transfers between devices: 97.1 us -> none  [factor_front(): pivot_all = lax.all_gather(pivot_piece[None], 'front', axis=0, tiled=True)]
    ppermute x0 -> x6, waiting for transfers between devices: none -> 86.2 us  [the longest x4 86.2 us: collect(): earlier.append(lax.ppermute(earlier[-1], axis, up))]
  transfers between devices with their start and end apart: 9 -> 13, of which waited for: 6 -> 7; matrix products, arithmetic and copies ran while one was open for 19% -> 20% of each run, Pallas kernels for 0% -> 0%
where the time goes in v1:
time: 1340 us; the launch traced here: 1320 us
  other arithmetic  614 us (46%)
  local copies, waits for them, and re-layouts  313 us (23%)
  waiting for transfers between devices  237 us (18%)
  matrix products  123 us (9%)
  between operations  25.6 us (2%)
    another operation x62, other arithmetic, factor_front(): lower_factor = jnp.linalg.cholesky(pivot_block)  346 us
    another operation x5, other arithmetic, factor_front(): lax.linalg.triangular_solve(lower_factor, coupling, left_side=False, lowe...  174 us
    all_gather x2, waiting for transfers between devices, factor_front(): lax.all_gather(panel_round.reshape(batch_count, local_tiles, TILE, S)[Non...  87.7 us
    ppermute x4, waiting for transfers between devices, collect(): earlier.append(lax.ppermute(earlier[-1], axis, up))  86.2 us
    another operation x30, matrix products, factor_front(): lax.linalg.triangular_solve(lower_factor, coupling, left_side=False, lowe...  63.6 us
    ppermute x5, waiting for transfers between devices, swapped(): return lax.ppermute(value, axis, pairs)  62.9 us
    another operation x53, local copies, waits for them, and re-layouts, factor_front(): lax.linalg.triangular_solve(lower_factor, coupling, left_side=False, lowe...  62.8 us
    another operation x28, matrix products, factor_front(): lower_factor = jnp.linalg.cholesky(pivot_block)  46.3 us
  transfers between devices with their start and end apart: 13, of which 7 were waited for; matrix products, arithmetic and copies ran while one was open for 20% of the time, Pallas kernels for 0%

profile of v1, /device:TPU:1, one launch (start us, length us, event | category | flops | bytes accessed | tf_op | source)
XLA Modules:
  0.0 1324.9 jit_solution(2814393110744437928)
XLA Ops:
  74.1 13.8 %select_add_fusion.1 = f32[1,4,256,16,256]{4,2,1,3,0:T(8,128)} fusion(bf16[16,4,256,256]{3,2,1,0:T(8,128)(2,1)} %gather_fusion.3, bf16[16,4,256,256]{3,2,1,0:T(8,128)(2,1)} %gather_fusion.1, pred[16]{0:T(512)(128)(4,1)S(1)} %and_bitcast_fusion.4, pred[16]{0:T(512)(128)(4,1)S(1)} %and_bitcast_fusion.6, pred[4,16]{0,1:T(8,128)(4,1)S(1)} %broadcast_and_fusion.2, ...), kind=kLoop, calls=%fused_computation.13 | loop fusion | flops 29360128 | bytes 33554592 | tf_op jit(solution)/shard_map/add | solution.py:128
  87.9 16.4 %copy.141 = f32[1,4,256,16,256]{2,4,3,1,0:T(8,128)} copy(f32[1,4,256,16,256]{4,2,1,3,0:T(8,128)} %select_add_fusion.1) | data formatting | bytes 33554432 | tf_op jit(solution)/shard_map/add | solution.py:128
  114.2 23.1 %collective-permute-done.2 = f32[1,1,1,256,1024]{3,4,2,1,0:T(8,128)} collective-permute-done((f32[1,1,1,256,1024]{3,4,2,1,0:T(8,128)}, f32[1,1,1,256,1024]{3,4,2,1,0:T(8,128)}, u32[]{:S(2)}, u32[]{:S(2)}) %collective-permute-start.2) | collective-permute-done | bytes 1048608 | tf_op jit(solution)/shard_map/ppermute | solution.py:21
  140.0 22.3 %collective-permute-done.3 = f32[1,1,1,256,1024]{3,4,2,1,0:T(8,128)} collective-permute-done((f32[1,1,1,256,1024]{3,4,2,1,0:T(8,128)}, f32[1,1,1,256,1024]{3,4,2,1,0:T(8,128)}, u32[]{:S(2)}, u32[]{:S(2)}) %collective-permute-start.3) | collective-permute-done | bytes 1048608 | tf_op jit(solution)/shard_map/ppermute | solution.py:21
  190.5 11.7 custom-call.91
  202.9 9.8 custom-call.92
  219.2 11.9 custom-call.93
  232.3 9.8 custom-call.94
  245.5 11.7 custom-call.95
  258.5 9.8 custom-call.96
  271.9 11.9 custom-call.97
  285.1 9.8 custom-call.98
  298.4 11.7 custom-call.99
  311.4 10.2 custom-call.100
  324.9 11.7 custom-call.101
  338.0 9.8 custom-call.102
  350.7 11.9 custom-call.103
  363.9 9.8 custom-call.104
  376.3 11.7 custom-call.105
  401.8 28.1 %while.4 = (s32[]{:T(128)}, f32[1,1024,1024]{2,1,0:T(8,128)}, s32[8,2]{0,1:T(2,128)S(1)}, f32[8,1,128,128]{3,2,1,0:T(8,128)}, s32[]{:T(128)}) while((s32[]{:T(128)}, f32[1,1024,1024]{2,1,0:T(8,128)}, s32[8,2]{0,1:T(2,128)S(1)}, f32[8,1,128,128]{3,2,1,0:T(8,128)}, s32[]{:T(128)}) %tuple.132), condition=%wide.while_cond, body=%wide.while_body.sunk | while | flops 2 | bytes 132205 | solution.py:92
  429.9 80.4 %custom-call.106 = f32[1,8,128,128]{2,3,1,0:T(8,128)} custom-call(f32[1,8,128,128]{3,2,1,0:T(8,128)} %bitcast.962), custom_call_target="InvertDiagBlocksLowerTriangular" | custom-call | tf_op jit(solution)/shard_map/triangular_solve/custom-call.7 | solution.py:92
  556.9 10.0 copy.151
  566.9 47.7 %all-gather.3.cloned.1.call-done = bf16[4,1,3,256,1024]{4,3,2,1,0:T(8,128)(2,1)} async-done(((bf16[1,1,3,256,1024]{4,3,2,1,0:T(8,128)(2,1)}), bf16[4,1,3,256,1024]{4,3,2,1,0:T(8,128)(2,1)}) %all-gather.3.cloned.1.call-update) | async-done | bytes 6291472 | tf_op jit(solution)/shard_map/all_gather | solution.py:96
  667.7 62.9 %collective-permute-done.5 = bf16[1,768,3072]{2,1,0:T(8,128)(2,1)} collective-permute-done((bf16[1,768,3072]{2,1,0:T(8,128)(2,1)}, bf16[1,768,3072]{2,1,0:T(8,128)(2,1)}, u32[]{:S(2)}, u32[]{:S(2)}) %collective-permute-start.5) | collective-permute-done | bytes 4718624 | tf_op jit(solution)/shard_map/ppermute | solution.py:31
  730.6 9.2 reshape_reshape.7
  766.2 13.8 %select_add_fusion = f32[1,4,256,16,256]{4,2,1,3,0:T(8,128)} fusion(bf16[16,4,256,256]{3,2,1,0:T(8,128)(2,1)} %gather_fusion.7, bf16[16,4,256,256]{3,2,1,0:T(8,128)(2,1)} %gather_fusion.5, pred[16]{0:T(512)(128)(4,1)S(1)} %and_bitcast_fusion, pred[16]{0:T(512)(128)(4,1)S(1)} %and_bitcast_fusion.2, pred[4,16]{0,1:T(8,128)(4,1)S(1)} %broadcast_and_fusion, ...), kind=kLoop, calls=%fused_computation.12 | loop fusion | flops 29360128 | bytes 33554592 | tf_op jit(solution)/shard_map/add | solution.py:142
  780.0 16.4 %copy.158 = f32[1,4,256,16,256]{2,4,3,1,0:T(8,128)} copy(f32[1,4,256,16,256]{4,2,1,3,0:T(8,128)} %select_add_fusion) | data formatting | bytes 33554432 | tf_op jit(solution)/shard_map/add | solution.py:142
  805.7 20.7 %collective-permute-done.8 = f32[1,1,1,256,1024]{3,4,2,1,0:T(8,128)} collective-permute-done((f32[1,1,1,256,1024]{3,4,2,1,0:T(8,128)}, f32[1,1,1,256,1024]{3,4,2,1,0:T(8,128)}, u32[]{:S(2)}, u32[]{:S(2)}) %collective-permute-start.8) | collective-permute-done | bytes 1048608 | tf_op jit(solution)/shard_map/ppermute | solution.py:21
  828.9 20.0 %collective-permute-done.9 = f32[1,1,1,256,1024]{3,4,2,1,0:T(8,128)} collective-permute-done((f32[1,1,1,256,1024]{3,4,2,1,0:T(8,128)}, f32[1,1,1,256,1024]{3,4,2,1,0:T(8,128)}, u32[]{:S(2)}, u32[]{:S(2)}) %collective-permute-start.9) | collective-permute-done | bytes 1048608 | tf_op jit(solution)/shard_map/ppermute | solution.py:21
  876.9 11.7 custom-call.111
  889.3 9.8 custom-call.112
  905.6 12.1 custom-call.113
  918.9 9.8 custom-call.114
  932.1 11.7 custom-call.115
  945.1 9.8 custom-call.116
  958.5 11.9 custom-call.117
  971.6 9.8 custom-call.118
  984.9 11.7 custom-call.119
  997.9 10.0 custom-call.120
  1011.2 11.7 custom-call.121
  1024.3 9.8 custom-call.122
  1037.0 12.1 custom-call.123
  1050.4 9.8 custom-call.124
  1062.9 11.7 custom-call.125
  1088.5 28.1 %while.5 = (s32[]{:T(128)}, f32[1,1024,1024]{2,1,0:T(8,128)}, s32[8,2]{0,1:T(2,128)S(1)}, f32[8,1,128,128]{3,2,1,0:T(8,128)}, s32[]{:T(128)}) while((s32[]{:T(128)}, f32[1,1024,1024]{2,1,0:T(8,128)}, s32[8,2]{0,1:T(2,128)S(1)}, f32[8,1,128,128]{3,2,1,0:T(8,128)}, s32[]{:T(128)}) %tuple.142), condition=%wide.while_cond.clone, body=%wide.while_body.clone.sunk | while | flops 2 | bytes 132205 | solution.py:92
  1116.6 80.2 %custom-call.126 = f32[1,8,128,128]{2,3,1,0:T(8,128)} custom-call(f32[1,8,128,128]{3,2,1,0:T(8,128)} %bitcast.961), custom_call_target="InvertDiagBlocksLowerTriangular" | custom-call | tf_op jit(solution)/shard_map/triangular_solve/custom-call.7 | solution.py:92
  1249.4 10.5 copy.167
  1265.9 40.0 %all-gather.5.cloned.1.call-done = bf16[4,1,3,256,1024]{4,3,2,1,0:T(8,128)(2,1)} async-done(((bf16[1,1,3,256,1024]{4,3,2,1,0:T(8,128)(2,1)}), bf16[4,1,3,256,1024]{4,3,2,1,0:T(8,128)(2,1)}) %all-gather.5.cloned.1.call-update) | async-done | bytes 6291472 | tf_op jit(solution)/shard_map/all_gather | solution.py:96
  (348 shorter events, 485.4 us)
Async XLA Ops:
  7.2 11.6 copy-start
  7.2 607.4 %all-gather.3.cloned.1.call-start = ((), (), s32[]{:S(2)}) async-start(), calls=%async_computation | async-start | bytes 7864320 | tf_op jit(solution)/shard_map/all_gather | solution.py:96
  8.7 10.4 copy-start.19
  8.7 10.8 copy-start.17
  8.7 10.8 copy-start.18
  8.7 95.5 %collective-permute-start.1 = (bf16[1,4,256,512]{2,3,1,0:T(8,128)(2,1)S(1)}, bf16[1,4,256,512]{2,3,1,0:T(8,128)(2,1)S(1)}, u32[]{:S(2)}, u32[]{:S(2)}) collective-permute-start(bf16[1,4,256,512]{2,3,1,0:T(8,128)(2,1)S(1)} %bitcast.955), channel_id=1, source_target_pairs={{0,4},{4,0},{8,12},{12,8},{16,20},{20,16},{24,28},{28,24},{32,36},... | collective-permute-start | bytes 3145736 | tf_op jit(solution)/shard_map/ppermute | solution.py:31
  18.7 29.1 %collective-permute-start = (bf16[1,3,256,3072]{2,3,1,0:T(8,128)(2,1)}, bf16[1,3,256,3072]{2,3,1,0:T(8,128)(2,1)}, u32[]{:S(2)}, u32[]{:S(2)}) collective-permute-start(bf16[1,3,256,3072]{2,3,1,0:T(8,128)(2,1)} %bitcast.918), channel_id=1, source_target_pairs={{0,4},{4,0},{8,12},{12,8},{16,20},{20,16},{24,28},{28,24},{32,36},... | collective-permute-start | bytes 14155784 | tf_op jit(solution)/shard_map/ppermute | solution.py:31
  108.6 1.9 copy-start.2
  111.5 26.0 %slice-start = ((f32[1,4,256,1024]{2,3,1,0:T(8,128)}), f32[1,3,256,1024]{2,3,1,0:T(8,128)S(1)}, s32[]{:S(2)}) async-start(f32[1,4,256,1024]{2,3,1,0:T(8,128)} %copy-done.2), calls=%async_computation.2 | async-start | bytes 6291456 | tf_op jit(solution)/shard_map/slice | solution.py:91
  111.5 25.8 %collective-permute-start.2 = (f32[1,1,1,256,1024]{3,4,2,1,0:T(8,128)}, f32[1,1,1,256,1024]{3,4,2,1,0:T(8,128)}, u32[]{:S(2)}, u32[]{:S(2)}) collective-permute-start(f32[1,1,1,256,1024]{3,4,2,1,0:T(8,128)} %slice_bitcast_fusion.5), channel_id=1, source_target_pairs={{0,1},{1,2},{2,3},{3,0},{4,5},{5,6},{6,7},{7,4},{8,9},{9,10},{10,1... | collective-permute-start | bytes 3145736 | tf_op jit(solution)/shard_map/ppermute | solution.py:21
  111.5 28.5 %collective-permute-start.4 = (f32[1,1,1,256,1024]{3,4,2,1,0:T(8,128)}, f32[1,1,1,256,1024]{3,4,2,1,0:T(8,128)}, u32[]{:S(2)}, u32[]{:S(2)}) collective-permute-start(f32[1,1,1,256,1024]{3,4,2,1,0:T(8,128)} %slice_bitcast_fusion.5), channel_id=1, source_target_pairs={{0,3},{1,0},{2,1},{3,2},{4,7},{5,4},{6,5},{7,6},{8,11},{9,8},{10,9... | collective-permute-start | bytes 3145736 | tf_op jit(solution)/shard_map/ppermute | solution.py:23
  137.3 25.0 %collective-permute-start.3 = (f32[1,1,1,256,1024]{3,4,2,1,0:T(8,128)}, f32[1,1,1,256,1024]{3,4,2,1,0:T(8,128)}, u32[]{:S(2)}, u32[]{:S(2)}) collective-permute-start(f32[1,1,1,256,1024]{3,4,2,1,0:T(8,128)} %collective-permute-done.2), channel_id=1, source_target_pairs={{0,1},{1,2},{2,3},{3,0},{4,5},{5,6},{6,7},{7,4},{8,9},{9,10},{10,1... | collective-permute-start | bytes 3145736 | tf_op jit(solution)/shard_map/ppermute | solution.py:21
  188.6 1.9 copy-start.10
  394.2 116.2 %copy-start.9 = (f32[1,3,256,1024]{3,2,1,0:T(8,128)S(1)}, f32[1,3,256,1024]{3,2,1,0:T(8,128)}, u32[]{:S(2)}) copy-start(f32[1,3,256,1024]{3,2,1,0:T(8,128)} %copy.147) | copy-start | bytes 9437188
  510.4 6.9 copy-start.14
  542.3 1.7 copy-start.4
  544.0 1.9 copy-start.16
  545.8 760.1 %all-gather.5.cloned.1.call-start = ((), (), s32[]{:S(2)}) async-start(), calls=%async_computation.1 | async-start | bytes 7864320 | tf_op jit(solution)/shard_map/all_gather | solution.py:96
  546.0 83.9 %collective-permute-start.6 = (bf16[1,4,256,256]{2,3,1,0:T(8,128)(2,1)S(1)}, bf16[1,4,256,256]{2,3,1,0:T(8,128)(2,1)S(1)}, u32[]{:S(2)}, u32[]{:S(2)}) collective-permute-start(bf16[1,4,256,256]{2,3,1,0:T(8,128)(2,1)S(1)} %bitcast.951), channel_id=1, source_target_pairs={{0,4},{4,0},{8,12},{12,8},{16,20},{20,16},{24,28},{28,24},{32,36},... | collective-permute-start | bytes 1572872 | tf_op jit(solution)/shard_map/ppermute | solution.py:31
  614.6 5.5 copy-start.12
  627.7 102.9 %collective-permute-start.5 = (bf16[1,768,3072]{2,1,0:T(8,128)(2,1)}, bf16[1,768,3072]{2,1,0:T(8,128)(2,1)}, u32[]{:S(2)}, u32[]{:S(2)}) collective-permute-start(bf16[1,768,3072]{2,1,0:T(8,128)(2,1)} %bitcast.954), channel_id=1, source_target_pairs={{0,8},{4,12},{8,0},{12,4},{16,24},{20,28},{24,16},{28,20},{32,40},... | collective-permute-start | bytes 14155784 | tf_op jit(solution)/shard_map/ppermute | solution.py:31
  631.3 165.1 %collective-permute-start.7 = (bf16[1,4,256,512]{2,3,1,0:T(8,128)(2,1)}, bf16[1,4,256,512]{2,3,1,0:T(8,128)(2,1)}, u32[]{:S(2)}, u32[]{:S(2)}) collective-permute-start(bf16[1,4,256,512]{2,3,1,0:T(8,128)(2,1)} %maximum_select_fusion.3), channel_id=1, source_target_pairs={{0,8},{4,12},{8,0},{12,4},{16,24},{20,28},{24,16},{28,20},{32,40},... | collective-permute-start | bytes 3145736 | tf_op jit(solution)/shard_map/ppermute | solution.py:31
  799.9 1.9 copy-start.3
  802.9 23.6 %slice-start.1 = ((f32[1,4,256,1024]{2,3,1,0:T(8,128)}), f32[1,3,256,1024]{2,3,1,0:T(8,128)S(1)}, s32[]{:S(2)}) async-start(f32[1,4,256,1024]{2,3,1,0:T(8,128)} %copy-done.3), calls=%async_computation.3 | async-start | bytes 6291456 | tf_op jit(solution)/shard_map/slice | solution.py:91
  802.9 23.5 %collective-permute-start.8 = (f32[1,1,1,256,1024]{3,4,2,1,0:T(8,128)}, f32[1,1,1,256,1024]{3,4,2,1,0:T(8,128)}, u32[]{:S(2)}, u32[]{:S(2)}) collective-permute-start(f32[1,1,1,256,1024]{3,4,2,1,0:T(8,128)} %slice_bitcast_fusion.2), channel_id=1, source_target_pairs={{0,1},{1,2},{2,3},{3,0},{4,5},{5,6},{6,7},{7,4},{8,9},{9,10},{10,1... | collective-permute-start | bytes 3145736 | tf_op jit(solution)/shard_map/ppermute | solution.py:21
  804.0 24.9 %collective-permute-start.10 = (f32[1,1,1,256,1024]{3,4,2,1,0:T(8,128)}, f32[1,1,1,256,1024]{3,4,2,1,0:T(8,128)}, u32[]{:S(2)}, u32[]{:S(2)}) collective-permute-start(f32[1,1,1,256,1024]{3,4,2,1,0:T(8,128)} %slice_bitcast_fusion.2), channel_id=1, source_target_pairs={{0,3},{1,0},{2,1},{3,2},{4,7},{5,4},{6,5},{7,6},{8,11},{9,8},{10,9... | collective-permute-start | bytes 3145736 | tf_op jit(solution)/shard_map/ppermute | solution.py:23
  826.5 22.5 %collective-permute-start.9 = (f32[1,1,1,256,1024]{3,4,2,1,0:T(8,128)}, f32[1,1,1,256,1024]{3,4,2,1,0:T(8,128)}, u32[]{:S(2)}, u32[]{:S(2)}) collective-permute-start(f32[1,1,1,256,1024]{3,4,2,1,0:T(8,128)} %collective-permute-done.8), channel_id=1, source_target_pairs={{0,1},{1,2},{2,3},{3,0},{4,5},{5,6},{6,7},{7,4},{8,9},{9,10},{10,1... | collective-permute-start | bytes 3145736 | tf_op jit(solution)/shard_map/ppermute | solution.py:21
  875.0 1.9 copy-start.11
  1080.9 115.9 %copy-start.8 = (f32[1,3,256,1024]{3,2,1,0:T(8,128)S(1)}, f32[1,3,256,1024]{3,2,1,0:T(8,128)}, u32[]{:S(2)}) copy-start(f32[1,3,256,1024]{3,2,1,0:T(8,128)} %copy.165) | copy-start | bytes 9437188
  1196.8 6.9 copy-start.15
  1228.7 1.7 copy-start.6
  1230.5 4.1 copy-start.5
  1249.4 10.5 copy-start.7
  1265.9 43.5 %copy-start.13 = (bf16[1,768,1024]{1,2,0:T(8,128)(2,1)S(1)}, bf16[1,768,1024]{1,2,0:T(8,128)(2,1)}, u32[]{:S(2)}) copy-start(bf16[1,768,1024]{1,2,0:T(8,128)(2,1)} %convert_element_type.105) | copy-start | bytes 4718596
  1309.4 8.3 copy-start.1
Sparse Core Ops, SparseCore 0:
  545.9 68.6 all-gather.2
  1234.7 71.1 all-gather.4
